TPU v7x, 128 devices: a whole 4x4x4 slice. The times are simulated.
128 devices in a mesh: rep: 32 (over x, z, core), layer: 4 (over y).
Axes of the slice: x: 4, y: 4, z: 4, core: 2. Of those that a mesh axis runs over, the one named last changes fastest.
Arguments:
- activations: bfloat16 [4, 16384, 8192], P('layer', 'rep'), may hold values from -6 to 6
- output_grads: bfloat16 [4, 16384, 8192], P('layer', 'rep'), may hold values from -6 to 6
- in_projection: bfloat16 [4, 32, 8192], P('layer'), may hold values from -0.0625 to 0.0625
- out_projection: bfloat16 [4, 32, 8192], P('layer'), may hold values from -0.0625 to 0.0625
- segment_ids: int32 [16384], P('rep'), may hold values from -1 to 61, as said below
- move_list: int32 [1984], P('rep'), may hold values from -1 to 1023, as said below
Outputs:
- factor: float32 [4, 1024, 1024], P('layer')
- features: bfloat16 [4, 1024, 1024], P('layer', 'rep')
- self_influence: float32 [1024], P('rep')
Inputs may be any that keep to these rules, and one draw needn't show every extreme that they name: `segment_ids`: within each replica's 512 tokens the values never fall; a run of equal values is one document; -1 marks tokens continuing the previous replica's last document and never occurs on replica 0; n documents start on a replica with values 0 to n - 1, n from 2 to 62, and some replica has exactly 62; all documents together are 1024; the last document ends at the end of the last replica. `move_list`: replica r's block of 62 entries gives for its documents in order of their first token (the one continuing onto replica r + 1 included) the destination row in 0 to 1023, and -1 past its last document; every row is named exactly once; the documents of replica r go to rows of replica r - 1, r or r + 1 (rows m * 32 to m * 32 + 31 belong to replica m).
All inputs are finite; a program needn't handle non-finite values.
Results may differ from a plain program's by a relative error of at most 0.0064.
Values may be sent and summed in bfloat16 or wider, within the bound.
A program may use at most 128 MiB of HBM per device.

v0:
```python
import jax
import jax.numpy as jnp
from jax import lax
from jax.sharding import PartitionSpec as P

BAL = 32
DAMPING = 0.05


def shifted(block, axis, distance):
    devices = range(lax.axis_size(axis))
    route = [(i - distance, i) for i in devices if i - distance in devices]
    return lax.ppermute(block, axis, route)


def on_device(activations, output_grads, in_projection, out_projection, segment_ids, move_list):
    contract = (((1,), (1,)), ((), ()))
    left = lax.dot_general(
        in_projection[0], activations[0], contract, preferred_element_type=jnp.float32
    ).astype(jnp.bfloat16)
    right = lax.dot_general(
        out_projection[0], output_grads[0], contract, preferred_element_type=jnp.float32
    ).astype(jnp.bfloat16)
    doc_slots = move_list.shape[0]
    width = left.shape[0] * right.shape[0]
    slot_ids = jnp.arange(doc_slots + 1, dtype=jnp.int32) - 1
    member = (segment_ids[None, :] == slot_ids[:, None]).astype(jnp.bfloat16)
    masked = member[:, None, :] * left[None, :, :]
    blocks = lax.dot_general(
        masked, right, (((2,), (1,)), ((), ())), preferred_element_type=jnp.float32
    )
    sums = blocks.reshape(doc_slots + 1, width)
    counts = jnp.sum(member.astype(jnp.float32), axis=1)
    carried_sum, carried_count = shifted((sums[:1], counts[:1]), "rep", -1)
    last_slot = jnp.max(segment_ids)
    takes = (slot_ids[1:] == last_slot).astype(jnp.float32)
    totals = sums[1:] + takes[:, None] * carried_sum
    lengths = counts[1:] + takes * carried_count[0]
    safe_len = jnp.maximum(lengths, 1.0)
    local_features = (totals / jnp.sqrt(safe_len)[:, None]).astype(jnp.bfloat16)
    replica = lax.axis_index("rep")
    n_rep = lax.axis_size("rep")
    offsets = jnp.where(move_list >= 0, move_list // BAL - replica, 5)
    within = move_list % BAL
    row_ids = jnp.arange(BAL, dtype=jnp.int32)

    def arrange(step_offset):
        select = ((offsets[None, :] == step_offset) & (within[None, :] == row_ids[:, None])).astype(
            jnp.bfloat16
        )
        return jnp.dot(select, local_features, preferred_element_type=jnp.float32).astype(
            jnp.bfloat16
        )

    staying = arrange(0)
    from_right = shifted(arrange(-1), "rep", -1)
    from_left = shifted(arrange(1), "rep", 1)
    mine = (
        staying.astype(jnp.float32) + from_right.astype(jnp.float32) + from_left.astype(jnp.float32)
    ).astype(jnp.bfloat16)
    rows_contract = (((0,), (0,)), ((), ()))
    local_gram = lax.dot_general(mine, mine, rows_contract, preferred_element_type=jnp.float32)
    gram = lax.psum(local_gram, "rep")
    total_docs = BAL * n_rep
    hessian = gram / total_docs + DAMPING * jnp.eye(width, dtype=jnp.float32)
    lower = jnp.linalg.cholesky(hessian)
    solved = lax.linalg.triangular_solve(
        lower, mine.T.astype(jnp.float32), left_side=True, lower=True
    )
    quad = jnp.sum(solved * solved, axis=0) / width
    influence = lax.psum(quad, "layer")
    return (lower.T[None], mine[None], influence)


def solution(mesh):
    placed = (
        P("layer", "rep", None),
        P("layer", "rep", None),
        P("layer", None, None),
        P("layer", None, None),
        P("rep"),
        P("rep"),
    )
    return jax.shard_map(
        on_device,
        mesh=mesh,
        in_specs=placed,
        out_specs=(P("layer", None, None), P("layer", "rep", None), P("rep")),
        check_vma=False,
    )
```

profile of v0, /device:TPU:6, one launch (start us, length us, event | category | flops | bytes accessed | tf_op | source)
XLA Modules:
  0.0 522.8 jit_solution(4648112741380501496)
XLA Ops:
  8.1 5.7 %collective-permute-start.1 = (f32[1]{0:T(128)S(1)}, f32[1]{0:T(128)}, u32[]{:S(2)}, u32[]{:S(2)}) collective-permute-start(f32[1]{0:T(128)S(1)} %bitcast.148), channel_id=1, source_target_pairs={{4,0},{8,4},{12,8},{16,12},{20,16},{24,20},{28,24},{32,28},{36,32}... | collective-permute-start | bytes 20 | tf_op jit(solution)/shard_map/ppermute | solution.py:13
  14.6 6.2 %fusion.10 = bf16[32,512]{1,0:T(8,128)(2,1)S(1)} fusion(bf16[1,512,8192]{2,1,0:T(8,128)(2,1)} %param.6, bf16[1,32,8192]{2,1,0:T(8,128)(2,1)} %param.8), kind=kOutput, calls=%fused_computation.33 | convolution fusion | flops 268451840 | bytes 8945664 | tf_op jit(solution)/shard_map/dot_general | solution.py:18
  20.8 6.7 %fusion.7 = f32[63,32,32]{2,1,0:T(8,128)S(1)} fusion(bf16[32,512]{1,0:T(8,128)(2,1)S(1)} %fusion.10, bf16[63,512]{1,0:T(8,128)(2,1)S(1)} %compare_convert_fusion, bf16[1,512,8192]{2,1,0:T(8,128)(2,1)} %param.7, bf16[1,32,8192]{2,1,0:T(8,128)(2,1)S(1)} %copy-done), kind=kOutput, calls=%fused_computation.14 | convolution fusion | flops 335544320 | bytes 9268224 | tf_op jit(solution)/shard_map/dot_general | solution.py:29
  36.2 5.8 %collective-permute-start.2 = (bf16[32,1024]{1,0:T(8,128)(2,1)S(1)}, bf16[32,1024]{1,0:T(8,128)(2,1)S(1)}, u32[]{:S(2)}, u32[]{:S(2)}) collective-permute-start(bf16[32,1024]{1,0:T(8,128)(2,1)S(1)} %convolution_convert_fusion.1), channel_id=1, source_target_pairs={{4,0},{8,4},{12,8},{16,12},{20,16},{24,20},{28,24},{32,28},{36,32}... | collective-permute-start | bytes 196616 | tf_op jit(solution)/shard_map/ppermute | solution.py:13
  43.9 2.8 fusion.102
  46.8 114.7 %all-reduce.3.cloned.1.call-done = f32[1024,1024]{0,1:T(8,128)} async-done(((f32[1024,1024]{0,1:T(8,128)}), f32[1024,1024]{0,1:T(8,128)}) %all-reduce.3.cloned.1.call-update) | async-done | bytes 4194320 | tf_op jit(solution)/shard_map/psum | solution.py:63
  161.5 5.1 select_add_fusion
  166.5 5.8 %copy.29 = f32[1024,1024]{1,0:T(8,128)} copy(f32[1024,1024]{0,1:T(8,128)} %select_add_fusion) | data formatting | bytes 8388608 | tf_op jit(solution)/shard_map/add | solution.py:65
  172.3 4.5 fusion.4
  178.8 11.7 %cholesky.222 = f32[128,128]{1,0:T(8,128)S(1)} custom-call(f32[128,128]{1,0:T(8,128)S(1)} %cholesky.577), custom_call_target="Cholesky" | custom-call | tf_op jit(solution)/shard_map/jit(cholesky)/cholesky | solution.py:66
  190.7 9.8 %custom-call.62 = f32[1,128,128]{1,2,0:T(8,128)S(1)} custom-call(f32[1,128,128]{2,1,0:T(8,128)S(1)} %get-tuple-element.48), custom_call_target="InvertDiagBlocksLowerTriangular" | custom-call | tf_op jit(solution)/shard_map/jit(cholesky)/cholesky | solution.py:66
  203.8 11.7 %cholesky.243 = f32[128,128]{1,0:T(8,128)S(1)} custom-call(f32[128,128]{1,0:T(8,128)S(1)} %cholesky.581), custom_call_target="Cholesky" | custom-call | tf_op jit(solution)/shard_map/jit(cholesky)/cholesky | solution.py:66
  215.8 9.8 %custom-call.63 = f32[1,128,128]{1,2,0:T(8,128)S(1)} custom-call(f32[1,128,128]{2,1,0:T(8,128)S(1)} %get-tuple-element.46), custom_call_target="InvertDiagBlocksLowerTriangular" | custom-call | tf_op jit(solution)/shard_map/jit(cholesky)/cholesky | solution.py:66
  231.1 11.7 %cholesky.466 = f32[128,128]{1,0:T(8,128)S(1)} custom-call(f32[128,128]{1,0:T(8,128)S(1)} %cholesky.586), custom_call_target="Cholesky" | custom-call | tf_op jit(solution)/shard_map/jit(cholesky)/cholesky | solution.py:66
  243.6 9.8 %custom-call.64 = f32[1,128,128]{1,2,0:T(8,128)S(1)} custom-call(f32[1,128,128]{2,1,0:T(8,128)S(1)} %get-tuple-element.44), custom_call_target="InvertDiagBlocksLowerTriangular" | custom-call | tf_op jit(solution)/shard_map/jit(cholesky)/cholesky | solution.py:66
  254.7 3.3 convolution_subtract_fusion.2
  258.1 11.7 %cholesky.485 = f32[128,128]{1,0:T(8,128)S(1)} custom-call(f32[128,128]{1,0:T(8,128)S(1)} %cholesky.591), custom_call_target="Cholesky" | custom-call | tf_op jit(solution)/shard_map/jit(cholesky)/cholesky | solution.py:66
  270.6 9.8 %custom-call.65 = f32[1,128,128]{1,2,0:T(8,128)S(1)} custom-call(f32[1,128,128]{2,1,0:T(8,128)S(1)} %get-tuple-element.42), custom_call_target="InvertDiagBlocksLowerTriangular" | custom-call | tf_op jit(solution)/shard_map/jit(cholesky)/cholesky | solution.py:66
  281.5 3.1 convolution_subtract_fusion.3
  284.7 12.1 %cholesky.504 = f32[128,128]{1,0:T(8,128)S(1)} custom-call(f32[128,128]{1,0:T(8,128)S(1)} %cholesky.596), custom_call_target="Cholesky" | custom-call | tf_op jit(solution)/shard_map/jit(cholesky)/cholesky | solution.py:66
  297.5 9.8 %custom-call.66 = f32[1,128,128]{1,2,0:T(8,128)S(1)} custom-call(f32[1,128,128]{2,1,0:T(8,128)S(1)} %get-tuple-element.40), custom_call_target="InvertDiagBlocksLowerTriangular" | custom-call | tf_op jit(solution)/shard_map/jit(cholesky)/cholesky | solution.py:66
  308.5 3.1 convolution_subtract_fusion.4
  311.6 11.7 %cholesky.524 = f32[128,128]{1,0:T(8,128)S(1)} custom-call(f32[128,128]{1,0:T(8,128)S(1)} %cholesky.601), custom_call_target="Cholesky" | custom-call | tf_op jit(solution)/shard_map/jit(cholesky)/cholesky | solution.py:66
  324.0 9.8 %custom-call.67 = f32[1,128,128]{1,2,0:T(8,128)S(1)} custom-call(f32[1,128,128]{2,1,0:T(8,128)S(1)} %get-tuple-element.38), custom_call_target="InvertDiagBlocksLowerTriangular" | custom-call | tf_op jit(solution)/shard_map/jit(cholesky)/cholesky | solution.py:66
  334.8 2.8 convolution_subtract_fusion.5
  337.7 11.7 %cholesky.544 = f32[128,128]{1,0:T(8,128)S(1)} custom-call(f32[128,128]{1,0:T(8,128)S(1)} %cholesky.606), custom_call_target="Cholesky" | custom-call | tf_op jit(solution)/shard_map/jit(cholesky)/cholesky | solution.py:66
  350.2 9.8 %custom-call.68 = f32[1,128,128]{1,2,0:T(8,128)S(1)} custom-call(f32[1,128,128]{2,1,0:T(8,128)S(1)} %get-tuple-element.36), custom_call_target="InvertDiagBlocksLowerTriangular" | custom-call | tf_op jit(solution)/shard_map/jit(cholesky)/cholesky | solution.py:66
  363.0 11.7 %cholesky.562 = f32[128,128]{1,0:T(8,128)S(1)} custom-call(f32[128,128]{1,0:T(8,128)S(1)} %convolution_subtract_fusion.6), custom_call_target="Cholesky" | custom-call | tf_op jit(solution)/shard_map/jit(cholesky)/cholesky | solution.py:66
  385.2 6.7 %fusion.5 = (f32[1024,1024]{0,1:T(8,128)}, f32[1,1024,1024]{2,1,0:T(8,128)}) fusion(f32[1024,1024]{0,1:T(8,128)} %constant_dynamic-update-slice_fusion.30, pred[]{:T(512)S(6)} %cholesky.576), kind=kLoop, calls=%fused_computation.12 | loop fusion | flops 4194304 | bytes 12582913 | tf_op jit(solution)/shard_map/triangular_solve | solution.py:67
  391.9 24.1 %while.1 = (s32[]{:T(128)}, f32[1024,1024]{0,1:T(8,128)}, s32[8,2]{0,1:T(2,128)S(1)}, f32[8,128,128]{2,1,0:T(8,128)S(1)}, s32[]{:T(128)}) while((s32[]{:T(128)}, f32[1024,1024]{0,1:T(8,128)}, s32[8,2]{0,1:T(2,128)S(1)}, f32[8,128,128]{2,1,0:T(8,128)S(1)}, s32[]{:T(128)}) %tuple.59), condition=%wide.while_cond, body=%wide.while_body.sunk | while | flops 2 | bytes 393329 | solution.py:67
  416.0 78.6 %custom-call.69 = f32[8,128,128]{1,2,0:T(8,128)S(1)} custom-call(f32[8,128,128]{2,1,0:T(8,128)S(1)} %get-tuple-element.10), custom_call_target="InvertDiagBlocksLowerTriangular" | custom-call | tf_op jit(solution)/shard_map/triangular_solve | solution.py:67
  504.7 11.0 %psum.15 = f32[32]{0:T(128)} all-reduce(f32[32]{0:T(128)S(1)} %broadcast_multiply_fusion), channel_id=1, replica_groups=mesh['rep'=32,'layer'=4] {'layer'}, use_global_device_ids=true, to_apply=%region_20.21 | all-reduce | flops 32 | bytes 256 | tf_op jit(solution)/shard_map/psum | solution.py:71
  (148 shorter events, 73.9 us)
Async XLA Ops:
  7.2 13.6 %copy-start = (bf16[1,32,8192]{2,1,0:T(8,128)(2,1)S(1)}, bf16[1,32,8192]{2,1,0:T(8,128)(2,1)}, u32[]{:S(2)}) copy-start(bf16[1,32,8192]{2,1,0:T(8,128)(2,1)} %param.9) | copy-start | bytes 1572868
  7.2 154.3 %all-reduce.3.cloned.1.call-start = ((), (), s32[]{:S(2)}) async-start(), calls=%async_computation | async-start | bytes 8388608 | tf_op jit(solution)/shard_map/psum | solution.py:63
  8.1 24.2 %collective-permute-start.1 = (f32[1]{0:T(128)S(1)}, f32[1]{0:T(128)}, u32[]{:S(2)}, u32[]{:S(2)}) collective-permute-start(f32[1]{0:T(128)S(1)} %bitcast.148), channel_id=1, source_target_pairs={{4,0},{8,4},{12,8},{16,12},{20,16},{24,20},{28,24},{32,28},{36,32}... | collective-permute-start | bytes 20 | tf_op jit(solution)/shard_map/ppermute | solution.py:13
  20.8 10.1 %copy-start.4 = (s32[512]{0:T(512)S(1)}, s32[512]{0:T(512)}, u32[]{:S(2)}) copy-start(s32[512]{0:T(512)} %param.10) | copy-start | bytes 6148
  20.8 11.5 %copy-start.5 = (s32[62]{0:T(128)S(1)}, s32[62]{0:T(128)}, u32[]{:S(2)}) copy-start(s32[62]{0:T(128)} %param.11) | copy-start | bytes 748
  27.6 6.2 %collective-permute-start = (f32[1,1024]{1,0:T(1,128)S(1)}, f32[1,1024]{1,0:T(1,128)S(1)}, u32[]{:S(2)}, u32[]{:S(2)}) collective-permute-start(f32[1,1024]{1,0:T(1,128)S(1)} %slice.248), channel_id=1, source_target_pairs={{4,0},{8,4},{12,8},{16,12},{20,16},{24,20},{28,24},{32,28},{36,32}... | collective-permute-start | bytes 12296 | tf_op jit(solution)/shard_map/ppermute | solution.py:13
  34.1 8.1 %collective-permute-start.3 = (bf16[32,1024]{1,0:T(8,128)(2,1)S(1)}, bf16[32,1024]{1,0:T(8,128)(2,1)S(1)}, u32[]{:S(2)}, u32[]{:S(2)}) collective-permute-start(bf16[32,1024]{1,0:T(8,128)(2,1)S(1)} %convolution_convert_fusion), channel_id=1, source_target_pairs={{0,4},{4,8},{8,12},{12,16},{16,20},{20,24},{24,28},{28,32},{32,36}... | collective-permute-start | bytes 196616 | tf_op jit(solution)/shard_map/ppermute | solution.py:13
  36.2 7.7 %collective-permute-start.2 = (bf16[32,1024]{1,0:T(8,128)(2,1)S(1)}, bf16[32,1024]{1,0:T(8,128)(2,1)S(1)}, u32[]{:S(2)}, u32[]{:S(2)}) collective-permute-start(bf16[32,1024]{1,0:T(8,128)(2,1)S(1)} %convolution_convert_fusion.1), channel_id=1, source_target_pairs={{4,0},{8,4},{12,8},{16,12},{20,16},{24,20},{28,24},{32,28},{36,32}... | collective-permute-start | bytes 196616 | tf_op jit(solution)/shard_map/ppermute | solution.py:13
  43.9 450.7 %copy-start.3 = (bf16[32,1024]{1,0:T(8,128)(2,1)}, bf16[32,1024]{1,0:T(8,128)(2,1)S(1)}, u32[]{:S(2)}) copy-start(bf16[32,1024]{1,0:T(8,128)(2,1)S(1)} %get-tuple-element.28) | copy-start | bytes 196612
  176.8 2.0 copy-start.2
  226.7 2.0 copy-start.1
Sparse Core Ops, SparseCore 0:
  46.9 114.5 all-reduce.2
where the time goes:
time: 530 us; the launch traced here: 523 us
  other arithmetic  267 us (50%)
  waiting for transfers between devices  116 us (22%)
  matrix products  51.9 us (10%)
  local copies, waits for them, and re-layouts  39.8 us (8%)
  between operations  19.9 us (4%)
  starting transfers between devices  16 us (3%)
  blocking collectives  11 us (2%)
    another operation x30, other arithmetic, on_device(): lower = jnp.linalg.cholesky(hessian)  168 us
    psum x1, waiting for transfers between devices, on_device(): gram = lax.psum(local_gram, 'rep')  115 us
    another operation x3, other arithmetic, on_device(): lax.linalg.triangular_solve(lower, mine.T.astype(jnp.float32), left_side=...  85.3 us
    another operation x14, matrix products, on_device(): lower = jnp.linalg.cholesky(hessian)  25.9 us
    another operation x40, local copies, waits for them, and re-layouts  23.6 us
    ppermute x4, starting transfers between devices, shifted(): return lax.ppermute(block, axis, route)  15.9 us
    psum x1, blocking collectives, on_device(): influence = lax.psum(quad, 'layer')  11 us
  transfers between devices with their start and end apart: 5, of which 2 were waited for; matrix products, arithmetic and copies ran while one was open for 3% of the time, Pallas kernels for 0%

commit v1 on v0

--- a/solution.py
+++ b/solution.py
@@ -60,7 +60,9 @@
     ).astype(jnp.bfloat16)
     rows_contract = (((0,), (0,)), ((), ()))
     local_gram = lax.dot_general(mine, mine, rows_contract, preferred_element_type=jnp.float32)
-    gram = lax.psum(local_gram, "rep")
+    gram = local_gram
+    for hop in (1, 2, 4, 8, 16):
+        gram = gram + lax.ppermute(gram, "rep", [(dev, dev ^ hop) for dev in range(32)])
     total_docs = BAL * n_rep
     hessian = gram / total_docs + DAMPING * jnp.eye(width, dtype=jnp.float32)
     lower = jnp.linalg.cholesky(hessian)

time: 530 us -> 789 us (1.49)
  waiting for transfers between devices: 116 us -> 375 us
  between operations: 19.9 us -> 6.55 us
  other arithmetic: 267 us -> 276 us
    ppermute x0 -> x5, waiting for transfers between devices: none -> 373 us  [on_device(): lax.ppermute(gram, 'rep', [(dev, dev ^ hop) for dev in range(32)])]
    psum x1 -> x0, waiting for transfers between devices: 115 us -> none  [on_device(): gram = lax.psum(local_gram, 'rep')]
  transfers between devices with their start and end apart: 5 -> 9, of which waited for: 2 -> 6; matrix products, arithmetic and copies ran while one was open for 3% -> 2% of each run, Pallas kernels for 0% -> 0%
where the time goes in v1:
time: 789 us; the launch traced here: 779 us
  waiting for transfers between devices  375 us (48%)
  other arithmetic  276 us (35%)
  matrix products  50 us (6%)
  local copies, waits for them, and re-layouts  39.2 us (5%)
  starting transfers between devices  20.5 us (3%)
  blocking collectives  11.3 us (1%)
    ppermute x5, waiting for transfers between devices, on_device(): lax.ppermute(gram, 'rep', [(dev, dev ^ hop) for dev in range(32)])  373 us
    another operation x30, other arithmetic, on_device(): lower = jnp.linalg.cholesky(hessian)  168 us
    another operation x3, other arithmetic, on_device(): lax.linalg.triangular_solve(lower, mine.T.astype(jnp.float32), left_side=...  85.3 us
    another operation x14, matrix products, on_device(): lower = jnp.linalg.cholesky(hessian)  26.1 us
    another operation x40, local copies, waits for them, and re-layouts  23.6 us
    ppermute x4, starting transfers between devices, shifted(): return lax.ppermute(block, axis, route)  15.9 us
  transfers between devices with their start and end apart: 9, of which 6 were waited for; matrix products, arithmetic and copies ran while one was open for 2% of the time, Pallas kernels for 0%

profile of v1, /device:TPU:6, one launch (start us, length us, event | category | flops | bytes accessed | tf_op | source)
XLA Modules:
  0.0 779.3 jit_solution(8234833383597549288)
XLA Ops:
  1.6 5.7 collective-permute-start.1
  8.0 6.2 fusion.10
  14.2 6.7 fusion.7
  29.7 5.8 collective-permute-start.2
  38.2 7.1 collective-permute-done.4
  46.8 92.6 %collective-permute-done.5 = f32[1024,1024]{0,1:T(8,128)S(1)} collective-permute-done((f32[1024,1024]{0,1:T(8,128)S(1)}, f32[1024,1024]{0,1:T(8,128)S(1)}, u32[]{:S(2)}, u32[]{:S(2)}) %collective-permute-start.5) | collective-permute-done | bytes 4194336 | tf_op jit(solution)/shard_map/ppermute | solution.py:65
  140.9 93.3 %collective-permute-done.6 = f32[1024,1024]{0,1:T(8,128)S(1)} collective-permute-done((f32[1024,1024]{0,1:T(8,128)S(1)}, f32[1024,1024]{0,1:T(8,128)S(1)}, u32[]{:S(2)}, u32[]{:S(2)}) %collective-permute-start.6) | collective-permute-done | bytes 4194336 | tf_op jit(solution)/shard_map/ppermute | solution.py:65
  237.5 90.0 %collective-permute-done.7 = f32[1024,1024]{0,1:T(8,128)S(1)} collective-permute-done((f32[1024,1024]{0,1:T(8,128)S(1)}, f32[1024,1024]{0,1:T(8,128)S(1)}, u32[]{:S(2)}, u32[]{:S(2)}) %collective-permute-start.7) | collective-permute-done | bytes 4194336 | tf_op jit(solution)/shard_map/ppermute | solution.py:65
  332.7 90.2 %collective-permute-done.8 = f32[1024,1024]{0,1:T(8,128)} collective-permute-done((f32[1024,1024]{0,1:T(8,128)}, f32[1024,1024]{0,1:T(8,128)}, u32[]{:S(2)}, u32[]{:S(2)}) %collective-permute-start.8) | collective-permute-done | bytes 4194336 | tf_op jit(solution)/shard_map/ppermute | solution.py:65
  422.9 6.9 select_add_fusion
  429.9 5.3 copy.31
  435.2 4.4 fusion.4
  441.7 11.7 %cholesky.222 = f32[128,128]{1,0:T(8,128)S(1)} custom-call(f32[128,128]{1,0:T(8,128)S(1)} %cholesky.577), custom_call_target="Cholesky" | custom-call | tf_op jit(solution)/shard_map/jit(cholesky)/cholesky | solution.py:68
  453.6 9.8 %custom-call.62 = f32[1,128,128]{1,2,0:T(8,128)S(1)} custom-call(f32[1,128,128]{2,1,0:T(8,128)S(1)} %get-tuple-element.48), custom_call_target="InvertDiagBlocksLowerTriangular" | custom-call | tf_op jit(solution)/shard_map/jit(cholesky)/cholesky | solution.py:68
  466.7 11.7 %cholesky.243 = f32[128,128]{1,0:T(8,128)S(1)} custom-call(f32[128,128]{1,0:T(8,128)S(1)} %cholesky.581), custom_call_target="Cholesky" | custom-call | tf_op jit(solution)/shard_map/jit(cholesky)/cholesky | solution.py:68
  478.9 9.8 %custom-call.63 = f32[1,128,128]{1,2,0:T(8,128)S(1)} custom-call(f32[1,128,128]{2,1,0:T(8,128)S(1)} %get-tuple-element.46), custom_call_target="InvertDiagBlocksLowerTriangular" | custom-call | tf_op jit(solution)/shard_map/jit(cholesky)/cholesky | solution.py:68
  494.3 11.7 %cholesky.466 = f32[128,128]{1,0:T(8,128)S(1)} custom-call(f32[128,128]{1,0:T(8,128)S(1)} %cholesky.586), custom_call_target="Cholesky" | custom-call | tf_op jit(solution)/shard_map/jit(cholesky)/cholesky | solution.py:68
  506.7 9.8 %custom-call.64 = f32[1,128,128]{1,2,0:T(8,128)S(1)} custom-call(f32[1,128,128]{2,1,0:T(8,128)S(1)} %get-tuple-element.44), custom_call_target="InvertDiagBlocksLowerTriangular" | custom-call | tf_op jit(solution)/shard_map/jit(cholesky)/cholesky | solution.py:68
  517.8 3.3 slice_subtract_fusion.2
  521.1 11.7 %cholesky.485 = f32[128,128]{1,0:T(8,128)S(1)} custom-call(f32[128,128]{1,0:T(8,128)S(1)} %cholesky.591), custom_call_target="Cholesky" | custom-call | tf_op jit(solution)/shard_map/jit(cholesky)/cholesky | solution.py:68
  533.6 9.8 %custom-call.65 = f32[1,128,128]{1,2,0:T(8,128)S(1)} custom-call(f32[1,128,128]{2,1,0:T(8,128)S(1)} %get-tuple-element.42), custom_call_target="InvertDiagBlocksLowerTriangular" | custom-call | tf_op jit(solution)/shard_map/jit(cholesky)/cholesky | solution.py:68
  547.7 11.9 %cholesky.504 = f32[128,128]{1,0:T(8,128)S(1)} custom-call(f32[128,128]{1,0:T(8,128)S(1)} %cholesky.596), custom_call_target="Cholesky" | custom-call | tf_op jit(solution)/shard_map/jit(cholesky)/cholesky | solution.py:68
  560.4 9.8 %custom-call.66 = f32[1,128,128]{1,2,0:T(8,128)S(1)} custom-call(f32[1,128,128]{2,1,0:T(8,128)S(1)} %get-tuple-element.40), custom_call_target="InvertDiagBlocksLowerTriangular" | custom-call | tf_op jit(solution)/shard_map/jit(cholesky)/cholesky | solution.py:68
  574.4 11.7 %cholesky.524 = f32[128,128]{1,0:T(8,128)S(1)} custom-call(f32[128,128]{1,0:T(8,128)S(1)} %cholesky.601), custom_call_target="Cholesky" | custom-call | tf_op jit(solution)/shard_map/jit(cholesky)/cholesky | solution.py:68
  586.9 9.8 %custom-call.67 = f32[1,128,128]{1,2,0:T(8,128)S(1)} custom-call(f32[1,128,128]{2,1,0:T(8,128)S(1)} %get-tuple-element.38), custom_call_target="InvertDiagBlocksLowerTriangular" | custom-call | tf_op jit(solution)/shard_map/jit(cholesky)/cholesky | solution.py:68
  600.8 11.7 %cholesky.544 = f32[128,128]{1,0:T(8,128)S(1)} custom-call(f32[128,128]{1,0:T(8,128)S(1)} %cholesky.606), custom_call_target="Cholesky" | custom-call | tf_op jit(solution)/shard_map/jit(cholesky)/cholesky | solution.py:68
  613.3 9.8 %custom-call.68 = f32[1,128,128]{1,2,0:T(8,128)S(1)} custom-call(f32[1,128,128]{2,1,0:T(8,128)S(1)} %get-tuple-element.36), custom_call_target="InvertDiagBlocksLowerTriangular" | custom-call | tf_op jit(solution)/shard_map/jit(cholesky)/cholesky | solution.py:68
  626.1 11.7 %cholesky.562 = f32[128,128]{1,0:T(8,128)S(1)} custom-call(f32[128,128]{1,0:T(8,128)S(1)} %slice_subtract_fusion.6), custom_call_target="Cholesky" | custom-call | tf_op jit(solution)/shard_map/jit(cholesky)/cholesky | solution.py:68
  648.3 6.7 fusion.5
  655.1 24.0 %while.1 = (s32[]{:T(128)}, f32[1024,1024]{0,1:T(8,128)}, s32[8,2]{0,1:T(2,128)S(1)}, f32[8,128,128]{2,1,0:T(8,128)S(1)}, s32[]{:T(128)}) while((s32[]{:T(128)}, f32[1024,1024]{0,1:T(8,128)}, s32[8,2]{0,1:T(2,128)S(1)}, f32[8,128,128]{2,1,0:T(8,128)S(1)}, s32[]{:T(128)}) %tuple.59), condition=%wide.while_cond, body=%wide.while_body.sunk | while | flops 2 | bytes 393329 | solution.py:69
  679.1 78.6 %custom-call.69 = f32[8,128,128]{1,2,0:T(8,128)S(1)} custom-call(f32[8,128,128]{2,1,0:T(8,128)S(1)} %get-tuple-element.10), custom_call_target="InvertDiagBlocksLowerTriangular" | custom-call | tf_op jit(solution)/shard_map/triangular_solve | solution.py:69
  767.8 11.3 %psum.7 = f32[32]{0:T(128)} all-reduce(f32[32]{0:T(128)S(1)} %broadcast_multiply_fusion), channel_id=1, replica_groups=mesh['rep'=32,'layer'=4] {'layer'}, use_global_device_ids=true, to_apply=%region_19.20 | all-reduce | flops 32 | bytes 256 | tf_op jit(solution)/shard_map/psum | solution.py:73
  (161 shorter events, 95.7 us)
Async XLA Ops:
  0.6 13.6 %copy-start = (bf16[1,32,8192]{2,1,0:T(8,128)(2,1)S(1)}, bf16[1,32,8192]{2,1,0:T(8,128)(2,1)}, u32[]{:S(2)}) copy-start(bf16[1,32,8192]{2,1,0:T(8,128)(2,1)} %param.9) | copy-start | bytes 1572868
  1.6 24.2 %collective-permute-start.1 = (f32[1]{0:T(128)S(1)}, f32[1]{0:T(128)}, u32[]{:S(2)}, u32[]{:S(2)}) collective-permute-start(f32[1]{0:T(128)S(1)} %bitcast.148), channel_id=1, source_target_pairs={{4,0},{8,4},{12,8},{16,12},{20,16},{24,20},{28,24},{32,28},{36,32}... | collective-permute-start | bytes 20 | tf_op jit(solution)/shard_map/ppermute | solution.py:13
  14.2 10.1 %copy-start.5 = (s32[512]{0:T(512)S(1)}, s32[512]{0:T(512)}, u32[]{:S(2)}) copy-start(s32[512]{0:T(512)} %param.10) | copy-start | bytes 6148
  14.2 11.5 %copy-start.6 = (s32[62]{0:T(128)S(1)}, s32[62]{0:T(128)}, u32[]{:S(2)}) copy-start(s32[62]{0:T(128)} %param.11) | copy-start | bytes 748
  21.0 6.2 collective-permute-start
  27.6 8.1 %collective-permute-start.3 = (bf16[32,1024]{1,0:T(8,128)(2,1)S(1)}, bf16[32,1024]{1,0:T(8,128)(2,1)S(1)}, u32[]{:S(2)}, u32[]{:S(2)}) collective-permute-start(bf16[32,1024]{1,0:T(8,128)(2,1)S(1)} %convolution_convert_fusion), channel_id=1, source_target_pairs={{0,4},{4,8},{8,12},{12,16},{16,20},{20,24},{24,28},{28,32},{32,36}... | collective-permute-start | bytes 196616 | tf_op jit(solution)/shard_map/ppermute | solution.py:13
  29.7 7.7 collective-permute-start.2
  37.4 720.3 %copy-start.4 = (bf16[32,1024]{1,0:T(8,128)(2,1)}, bf16[32,1024]{1,0:T(8,128)(2,1)S(1)}, u32[]{:S(2)}) copy-start(bf16[32,1024]{1,0:T(8,128)(2,1)S(1)} %get-tuple-element.28) | copy-start | bytes 196612
  38.1 7.2 collective-permute-start.4
  46.7 92.7 %collective-permute-start.5 = (f32[1024,1024]{0,1:T(8,128)S(1)}, f32[1024,1024]{0,1:T(8,128)S(1)}, u32[]{:S(2)}, u32[]{:S(2)}) collective-permute-start(f32[1024,1024]{0,1:T(8,128)S(1)} %add.125), channel_id=1, source_target_pairs={{0,8},{4,12},{8,0},{12,4},{16,24},{20,28},{24,16},{28,20},{32,40},... | collective-permute-start | bytes 12582920 | tf_op jit(solution)/shard_map/ppermute | solution.py:65
  140.8 93.4 %collective-permute-start.6 = (f32[1024,1024]{0,1:T(8,128)S(1)}, f32[1024,1024]{0,1:T(8,128)S(1)}, u32[]{:S(2)}, u32[]{:S(2)}) collective-permute-start(f32[1024,1024]{0,1:T(8,128)S(1)} %add.126), channel_id=1, source_target_pairs={{0,16},{4,20},{8,24},{12,28},{16,0},{20,4},{24,8},{28,12},{32,48},... | collective-permute-start | bytes 12582920 | tf_op jit(solution)/shard_map/ppermute | solution.py:65
  235.5 91.9 %collective-permute-start.7 = (f32[1024,1024]{0,1:T(8,128)S(1)}, f32[1024,1024]{0,1:T(8,128)S(1)}, u32[]{:S(2)}, u32[]{:S(2)}) collective-permute-start(f32[1024,1024]{0,1:T(8,128)S(1)} %add.127), channel_id=1, source_target_pairs={{0,32},{4,36},{8,40},{12,44},{16,48},{20,52},{24,56},{28,60},{32,0... | collective-permute-start | bytes 12582920 | tf_op jit(solution)/shard_map/ppermute | solution.py:65
  330.4 92.6 %collective-permute-start.8 = (f32[1024,1024]{0,1:T(8,128)}, f32[1024,1024]{0,1:T(8,128)}, u32[]{:S(2)}, u32[]{:S(2)}) collective-permute-start(f32[1024,1024]{0,1:T(8,128)} %add.128), channel_id=1, source_target_pairs={{0,64},{4,68},{8,72},{12,76},{16,80},{20,84},{24,88},{28,92},{32,9... | collective-permute-start | bytes 12582920 | tf_op jit(solution)/shard_map/ppermute | solution.py:65
  439.7 2.0 copy-start.3
  489.9 2.0 copy-start.2
  648.3 130.8 %copy-start.1 = (bf16[1,32,8192]{2,1,0:T(8,128)(2,1)S(1)}, bf16[1,32,8192]{2,1,0:T(8,128)(2,1)}, u32[]{:S(2)}) copy-start(bf16[1,32,8192]{2,1,0:T(8,128)(2,1)} %param.9) | copy-start | bytes 1572868
